TPU v7x, 512 devices: a whole 4x4x16 slice. The times are simulated.
512 devices in a mesh: ctx: 16 (over y, x), head: 32 (over z, core).
Axes of the slice: x: 4, y: 4, z: 16, core: 2. Of those that a mesh axis runs over, the one named last changes fastest.
Arguments:
- doc_lengths: int32 [4], replicated, may hold values from 1 to 6144, 8192 in all
- lin_q: bfloat16 [8192, 8192], P('ctx', 'head'), may hold values from -6 to 6
- lin_k: bfloat16 [8192, 8192], P('ctx', 'head'), may hold values from -6 to 6
- lin_v: bfloat16 [8192, 8192], P('ctx', 'head'), may hold values from -40 to 40
- log_decay: float32 [64, 8192], P('head', 'ctx'), may hold values from -1 to 0
- lin_gain: float32 [8192], P('head'), may hold values from 0.5 to 1.5
- soft_q: bfloat16 [8192, 8192], P('ctx', 'head'), may hold values from -48 to 48
- soft_k: bfloat16 [8192, 1024], P('ctx', 'head'), may hold values from -6 to 6
- soft_v: bfloat16 [8192, 1024], P('ctx', 'head'), may hold values from -6 to 6
Outputs:
- lin_out: bfloat16 [8192, 8192], P('ctx', 'head')
- soft_out: bfloat16 [8192, 8192], P('ctx', 'head')
Inputs may be any that keep to these rules, and one draw needn't show every extreme that they name: `doc_lengths`: the 4 lengths sum to 8192 and the largest is exactly 6144.
All inputs are finite; a program needn't handle non-finite values.
Results may differ from a plain program's by a relative error of at most 0.015.
Values may be sent and summed in bfloat16 or wider, within the bound.
A program may use at most 64 MiB of HBM per device.

v0:
```python
import jax
import jax.numpy as jnp
from jax import lax
from jax.sharding import PartitionSpec as P

KVH = 8
DH = 128
BLK = 256


def prefix(value, axis, join, neutral):
    place = lax.axis_index(axis)
    gathered = jax.tree.map(
        lambda a, kind: lax.all_gather(a.astype(kind), axis), value, (jnp.bfloat16, jnp.bfloat16)
    )
    state = jax.tree.map(lambda a, e: jnp.zeros_like(a) + jnp.asarray(e, a.dtype), value, neutral)

    def one(turn, state):
        return join(
            state,
            jax.tree.map(
                lambda a, own: lax.dynamic_index_in_dim(a, turn, 0, False).astype(own.dtype),
                gathered,
                value,
            ),
        )

    return lax.fori_loop(0, place, one, state)


def swapped(value, axis, stride):
    return lax.ppermute(value, axis, [(i, i ^ 1 << stride) for i in range(lax.axis_size(axis))])


def doc_index(doc_lengths, positions):
    bounds = jnp.cumsum(doc_lengths)
    counted = jnp.sum((bounds[None, :] <= positions[:, None]).astype(jnp.int32), axis=1)
    return jnp.where(positions < 0, -1, counted)


def lightning_parts(queries, keys_block, values_block, decay_block, segs_block, seg_before):
    running = jnp.cumsum(decay_block, axis=1)
    block_len = segs_block.shape[0]
    rows_iota = lax.broadcasted_iota(jnp.int32, (block_len, block_len), 0)
    cols_iota = lax.broadcasted_iota(jnp.int32, (block_len, block_len), 1)
    allowed = (rows_iota >= cols_iota) & (segs_block[:, None] == segs_block[None, :])
    spread = jnp.where(allowed[None], running[:, :, None] - running[:, None, :], 0.0)
    decays = jnp.where(allowed[None], jnp.exp(spread), 0.0)
    scores = (
        jnp.einsum("ihd,jhd->hij", queries, keys_block, preferred_element_type=jnp.float32) * decays
    )
    scores = scores.astype(jnp.bfloat16)
    inside = jnp.einsum("hij,jhd->ihd", scores, values_block, preferred_element_type=jnp.float32)
    carried = (segs_block == seg_before).astype(jnp.float32)
    entering = jnp.exp(running) * carried[None, :]
    closing = running[:, -1:]
    tail_mask = (segs_block == segs_block[-1]).astype(jnp.float32)
    weights = jnp.exp(closing - running) * tail_mask[None, :]
    weighted = (keys_block * weights.T[:, :, None]).astype(jnp.bfloat16)
    update = jnp.einsum("jhd,jhe->hde", weighted, values_block, preferred_element_type=jnp.float32)
    kept_flag = (segs_block[-1] == seg_before).astype(jnp.float32)
    decay_factor = kept_flag * jnp.exp(closing[:, 0])
    return (inside, entering, update, decay_factor)


def local(doc_lengths, lin_q, lin_k, lin_v, log_decay, lin_gain, soft_q, soft_k, soft_v):
    tok_count = lin_q.shape[0]
    heads_here = lin_gain.shape[0] // DH
    ctx_place = lax.axis_index("ctx")
    positions = ctx_place * tok_count + jnp.arange(tok_count, dtype=jnp.int32)
    doc_ids = doc_index(doc_lengths, positions)
    seg_previous = doc_index(doc_lengths, positions[:1] - 1)[0]
    query_rows = lin_q.reshape(tok_count, heads_here, DH)
    key_rows = lin_k.reshape(tok_count, heads_here, DH)
    value_rows = lin_v.reshape(tok_count, heads_here, DH)
    blocks = tok_count // BLK
    pieces_list = []
    local_state = jnp.zeros((heads_here, DH, DH), jnp.float32)
    through = jnp.ones((heads_here,), jnp.float32)
    for number in range(blocks):
        first_row = number * BLK
        last_row = first_row + BLK
        seg_before = seg_previous if number == 0 else doc_ids[first_row - 1]
        parts_now = lightning_parts(
            query_rows[first_row:last_row],
            key_rows[first_row:last_row],
            value_rows[first_row:last_row],
            log_decay[:, first_row:last_row],
            doc_ids[first_row:last_row],
            seg_before,
        )
        pieces_list.append(parts_now)
        local_state = parts_now[3][:, None, None] * local_state + parts_now[2]
        through = through * parts_now[3]
    empty_state = jnp.zeros((heads_here, DH, DH), jnp.float32)

    def combine(earlier, later):
        return (earlier[0] * later[0], later[0][:, None, None] * earlier[1] + later[1])

    incoming = prefix(
        (through, local_state), "ctx", combine, (jnp.ones((heads_here,), jnp.float32), empty_state)
    )
    carry_state = incoming[1]
    outputs = []
    for number in range(blocks):
        first_row = number * BLK
        inside, entering, update, decay_factor = pieces_list[number]
        across = jnp.einsum(
            "ihd,hde->ihe",
            query_rows[first_row : first_row + BLK],
            carry_state.astype(jnp.bfloat16),
            preferred_element_type=jnp.float32,
        )
        outputs.append(inside + across * entering.T[:, :, None])
        carry_state = decay_factor[:, None, None] * carry_state + update
    raw_out = jnp.concatenate(outputs, axis=0)
    norm_scale = lax.rsqrt(jnp.mean(raw_out * raw_out, axis=2, keepdims=True) + 1e-06)
    lin_out = (
        (raw_out * norm_scale * lin_gain.reshape(1, heads_here, DH))
        .reshape(tok_count, heads_here * DH)
        .astype(jnp.bfloat16)
    )
    head_place = lax.axis_index("head")
    group_width = lax.axis_size("head") // KVH
    bit_count = group_width.bit_length() - 1
    own_keys, own_values = (soft_k, soft_v)
    for bit in range(bit_count):
        far_keys, far_values = swapped((own_keys, own_values), "head", bit)
        upper = head_place // (1 << bit) % 2 == 1
        own_keys = jnp.where(
            upper,
            jnp.concatenate([far_keys, own_keys], axis=1),
            jnp.concatenate([own_keys, far_keys], axis=1),
        )
        own_values = jnp.where(
            upper,
            jnp.concatenate([far_values, own_values], axis=1),
            jnp.concatenate([own_values, far_values], axis=1),
        )
    soft_rows = soft_q.reshape(tok_count, heads_here, DH)

    def attend(softmax_state, key_piece, value_piece, key_start):
        row_top, row_total, accum_rows = softmax_state
        key_pos = key_start + jnp.arange(key_piece.shape[0], dtype=jnp.int32)
        key_doc = doc_index(doc_lengths, key_pos)
        scores = jnp.einsum(
            "ihd,jd->hij", soft_rows, key_piece, preferred_element_type=jnp.float32
        ) * DH ** (-0.5)
        allowed = (key_pos[None, :] <= positions[:, None]) & (key_doc[None, :] == doc_ids[:, None])
        masked = jnp.where(allowed[None], scores, -1e30)
        new_top = jnp.maximum(row_top, jnp.max(masked, axis=2))
        exp_terms = jnp.where(allowed[None], jnp.exp(scores - new_top[:, :, None]), 0.0)
        rescale = jnp.exp(row_top - new_top)
        new_total = rescale * row_total + jnp.sum(exp_terms, axis=2)
        new_accum = rescale[:, :, None] * accum_rows + jnp.einsum(
            "hij,jd->hid",
            exp_terms.astype(jnp.bfloat16),
            value_piece,
            preferred_element_type=jnp.float32,
        )
        return (new_top, new_total, new_accum)

    def visit(softmax_state, key_piece, value_piece, key_start):
        return attend(softmax_state, key_piece, value_piece, key_start)

    start_state = (
        jnp.full((heads_here, tok_count), -1e30, jnp.float32),
        jnp.zeros((heads_here, tok_count), jnp.float32),
        jnp.zeros((heads_here, tok_count, DH), jnp.float32),
    )
    key_piece = lax.all_gather(own_keys, "ctx", axis=0, tiled=True)
    value_piece = lax.all_gather(own_values, "ctx", axis=0, tiled=True)
    row_count = key_piece.shape[0]

    def inner_visit(state_in, scan_items):
        offset, key_part, value_part = scan_items
        return (visit(state_in, key_part, value_part, offset), None)

    offsets = jnp.arange(row_count // 512, dtype=jnp.int32) * 512
    result, _ = lax.scan(
        inner_visit,
        start_state,
        (
            offsets,
            key_piece.reshape(row_count // 512, 512, DH),
            value_piece.reshape(row_count // 512, 512, DH),
        ),
    )
    final_top, final_total, final_accum = result
    soft_out = (
        (final_accum / final_total[:, :, None])
        .transpose(1, 0, 2)
        .reshape(tok_count, heads_here * DH)
        .astype(jnp.bfloat16)
    )
    return (lin_out, soft_out)


def solution(mesh):
    placed = (
        P(),
        P("ctx", "head"),
        P("ctx", "head"),
        P("ctx", "head"),
        P("head", "ctx"),
        P("head"),
        P("ctx", "head"),
        P("ctx", "head"),
        P("ctx", "head"),
    )
    return jax.shard_map(
        local,
        mesh=mesh,
        in_specs=placed,
        out_specs=(P("ctx", "head"), P("ctx", "head")),
        check_vma=False,
    )
```

profile of v0, /device:TPU:1, one launch (start us, length us, event | category | flops | bytes accessed | tf_op | source)
XLA Modules:
  0.0 323.4 jit_solution(9549522584730469660)
XLA Ops:
  21.5 8.8 %collective-permute-start = (bf16[512,32]{0,1:T(8,128)(2,1)S(1)}, bf16[512,32]{0,1:T(8,128)(2,1)S(1)}, u32[]{:S(2)}, u32[]{:S(2)}) collective-permute-start(bf16[512,32]{0,1:T(8,128)(2,1)S(1)} %copy-done.2), channel_id=1, source_target_pairs={{0,1},{1,0},{2,3},{3,2},{4,5},{5,4},{6,7},{7,6},{8,9},{9,8},{10,11... | collective-permute-start | bytes 98312 | tf_op jit(solution)/shard_map/ppermute | solution.py:32
  31.1 1.9 collective-permute-start.1
  33.1 3.1 collective-permute-done.1
  36.9 3.4 %collective-permute-start.2 = (bf16[512,32]{0,1:T(8,128)(2,1)S(1)}, bf16[512,32]{0,1:T(8,128)(2,1)S(1)}, u32[]{:S(2)}, u32[]{:S(2)}) collective-permute-start(bf16[512,32]{0,1:T(8,128)(2,1)S(1)} %copy-done.3), channel_id=1, source_target_pairs={{0,1},{1,0},{2,3},{3,2},{4,5},{5,4},{6,7},{7,6},{8,9},{9,8},{10,11... | collective-permute-start | bytes 98312 | tf_op jit(solution)/shard_map/ppermute | solution.py:32
  41.2 1.9 collective-permute-start.3
  43.1 3.1 collective-permute-done.3
  49.1 28.6 %all-reduce = bf16[32]{0:T(256)(128)(2,1)S(1)} all-reduce(bf16[32]{0:T(256)(128)(2,1)S(1)} %dynamic-update-slice), channel_id=2, replica_groups=mesh['ctx'=16,'head'=32] {'ctx'}, use_global_device_ids=true, to_apply=%add | all-reduce | flops 32 | bytes 128
  78.7 4.9 %all-gather.10.cloned.1.call-done = bf16[32,128,128]{2,1,0:T(8,128)(2,1)} async-done(((bf16[2,128,128]{2,1,0:T(8,128)(2,1)}), bf16[32,128,128]{2,1,0:T(8,128)(2,1)}) %all-gather.10.cloned.1.call-update) | async-done | bytes 1048592 | tf_op jit(solution)/shard_map/all_gather | solution.py:14
  87.0 62.9 %all-gather.6.cloned.1.call-done = bf16[8192,128]{0,1:T(8,128)(2,1)} async-done(((bf16[512,128]{0,1:T(8,128)(2,1)}), bf16[8192,128]{0,1:T(8,128)(2,1)}) %all-gather.6.cloned.1.call-update) | async-done | bytes 2097168 | tf_op jit(solution)/shard_map/all_gather | solution.py:171
  150.0 4.1 %copy.122 = bf16[8192,128]{1,0:T(8,128)(2,1)} copy(bf16[8192,128]{0,1:T(8,128)(2,1)} %all-gather.6.cloned.1.call-done) | data formatting | bytes 4194304 | tf_op jit(solution)/shard_map/all_gather | solution.py:171
  154.1 61.4 %all-gather.8.cloned.1.call-done = bf16[8192,128]{0,1:T(8,128)(2,1)} async-done(((bf16[512,128]{0,1:T(8,128)(2,1)}), bf16[8192,128]{0,1:T(8,128)(2,1)}) %all-gather.8.cloned.1.call-update) | async-done | bytes 2097168 | tf_op jit(solution)/shard_map/all_gather | solution.py:172
  215.5 4.1 %copy.124 = bf16[8192,128]{1,0:T(8,128)(2,1)} copy(bf16[8192,128]{0,1:T(8,128)(2,1)} %all-gather.8.cloned.1.call-done) | data formatting | bytes 4194304 | tf_op jit(solution)/shard_map/all_gather | solution.py:172
  219.5 96.5 %while.30 = (s32[]{:T(128)}, f32[2,512]{1,0:T(2,128)S(1)}, f32[2,512]{1,0:T(2,128)S(1)}, f32[2,512,128]{2,1,0:T(8,128)S(1)}, s32[16]{0:T(128)S(1)}, /*index=5*/s...) while((s32[]{:T(128)}, f32[2,512]{1,0:T(2,128)S(1)}, ...), condition=%wide.region_15.16_spmd.clone, body=%wide.region_11.15_spmd.clone.sunk | while | flops 275395584 | bytes 9000113 | solution.py:180
  221.8 1.5 fusion.92
  223.8 1.7 convolution_add_fusion.3
  229.8 1.7 convolution_add_fusion.3
  235.9 1.7 convolution_add_fusion.3
  239.9 1.5 fusion.92
  241.9 1.7 convolution_add_fusion.3
  247.9 1.7 convolution_add_fusion.3
  253.9 1.7 convolution_add_fusion.3
  258.0 1.5 fusion.92
  260.0 1.7 convolution_add_fusion.3
  266.0 1.7 convolution_add_fusion.3
  272.0 1.7 convolution_add_fusion.3
  278.1 1.7 convolution_add_fusion.3
  284.1 1.7 convolution_add_fusion.3
  290.1 1.7 convolution_add_fusion.3
  296.2 1.7 convolution_add_fusion.3
  302.2 1.7 convolution_add_fusion.3
  308.2 1.7 convolution_add_fusion.3
  314.2 1.7 convolution_add_fusion.3
  (247 shorter events, 83.9 us)
Async XLA Ops:
  7.2 14.3 %copy-start.2 = (bf16[512,32]{0,1:T(8,128)(2,1)S(1)}, bf16[512,32]{0,1:T(8,128)(2,1)}, u32[]{:S(2)}) copy-start(bf16[512,32]{0,1:T(8,128)(2,1)} %param.20) | copy-start | bytes 98308
  7.2 29.7 %copy-start.3 = (bf16[512,32]{0,1:T(8,128)(2,1)S(1)}, bf16[512,32]{0,1:T(8,128)(2,1)}, u32[]{:S(2)}) copy-start(bf16[512,32]{0,1:T(8,128)(2,1)} %param.21) | copy-start | bytes 98308
  7.2 76.5 %all-gather.10.cloned.1.call-start = ((), (), s32[]{:S(2)}) async-start(), calls=%async_computation.2 | async-start | bytes 1114112 | tf_op jit(solution)/shard_map/all_gather | solution.py:14
  17.8 59.9 %copy-start = (bf16[512,256]{1,0:T(8,128)(2,1)S(1)}, bf16[512,256]{1,0:T(8,128)(2,1)}, u32[]{:S(2)}) copy-start(bf16[512,256]{1,0:T(8,128)(2,1)} %param.19) | copy-start | bytes 786436
  19.9 58.1 %copy-start.5 = (s32[4]{0:T(128)S(1)}, s32[4]{0:T(128)}, u32[]{:S(2)}) copy-start(s32[4]{0:T(128)} %param.13) | copy-start | bytes 52
  19.9 58.4 %copy-start.1 = (bf16[512,256]{1,0:T(8,128)(2,1)S(1)}, bf16[512,256]{1,0:T(8,128)(2,1)}, u32[]{:S(2)}) copy-start(bf16[512,256]{1,0:T(8,128)(2,1)} %param.14) | copy-start | bytes 786436
  21.4 128.6 %all-gather.6.cloned.1.call-start = ((), (), s32[]{:S(2)}) async-start(), calls=%async_computation | async-start | bytes 2228224 | tf_op jit(solution)/shard_map/all_gather | solution.py:171
  21.5 9.6 %collective-permute-start = (bf16[512,32]{0,1:T(8,128)(2,1)S(1)}, bf16[512,32]{0,1:T(8,128)(2,1)S(1)}, u32[]{:S(2)}, u32[]{:S(2)}) collective-permute-start(bf16[512,32]{0,1:T(8,128)(2,1)S(1)} %copy-done.2), channel_id=1, source_target_pairs={{0,1},{1,0},{2,3},{3,2},{4,5},{5,4},{6,7},{7,6},{8,9},{9,8},{10,11... | collective-permute-start | bytes 98312 | tf_op jit(solution)/shard_map/ppermute | solution.py:32
  31.1 5.0 %collective-permute-start.1 = (bf16[512,64]{0,1:T(8,128)(2,1)S(1)}, bf16[512,64]{0,1:T(8,128)(2,1)S(1)}, u32[]{:S(2)}, u32[]{:S(2)}) collective-permute-start(bf16[512,64]{0,1:T(8,128)(2,1)S(1)} %maximum_select_fusion.2), channel_id=1, source_target_pairs={{0,2},{1,3},{2,0},{3,1},{4,6},{5,7},{6,4},{7,5},{8,10},{9,11},{10,... | collective-permute-start | bytes 196616 | tf_op jit(solution)/shard_map/ppermute | solution.py:32
  36.8 178.6 %all-gather.8.cloned.1.call-start = ((), (), s32[]{:S(2)}) async-start(), calls=%async_computation.1 | async-start | bytes 2228224 | tf_op jit(solution)/shard_map/all_gather | solution.py:172
  36.9 4.3 %collective-permute-start.2 = (bf16[512,32]{0,1:T(8,128)(2,1)S(1)}, bf16[512,32]{0,1:T(8,128)(2,1)S(1)}, u32[]{:S(2)}, u32[]{:S(2)}) collective-permute-start(bf16[512,32]{0,1:T(8,128)(2,1)S(1)} %copy-done.3), channel_id=1, source_target_pairs={{0,1},{1,0},{2,3},{3,2},{4,5},{5,4},{6,7},{7,6},{8,9},{9,8},{10,11... | collective-permute-start | bytes 98312 | tf_op jit(solution)/shard_map/ppermute | solution.py:32
  41.2 5.0 %collective-permute-start.3 = (bf16[512,64]{0,1:T(8,128)(2,1)S(1)}, bf16[512,64]{0,1:T(8,128)(2,1)S(1)}, u32[]{:S(2)}, u32[]{:S(2)}) collective-permute-start(bf16[512,64]{0,1:T(8,128)(2,1)S(1)} %maximum_select_fusion.3), channel_id=1, source_target_pairs={{0,2},{1,3},{2,0},{3,1},{4,6},{5,7},{6,4},{7,5},{8,10},{9,11},{10,... | collective-permute-start | bytes 196616 | tf_op jit(solution)/shard_map/ppermute | solution.py:32
  84.7 1.6 copy-start.4
Sparse Core Ops, SparseCore 0:
  21.5 62.0 all-gather.9
  87.2 62.7 all-gather.5
  153.0 62.4 all-gather.7
where the time goes:
time: 326 us; the launch traced here: 323 us
  waiting for transfers between devices  137 us (42%)
  matrix products  53.5 us (16%)
  other arithmetic  43.1 us (13%)
  blocking collectives  28.6 us (9%)
  local copies, waits for them, and re-layouts  25.8 us (8%)
  between operations  18.1 us (6%)
  starting transfers between devices  16.2 us (5%)
    all_gather x1, waiting for transfers between devices, local(): key_piece = lax.all_gather(own_keys, 'ctx', axis=0, tiled=True)  62.9 us
    all_gather x1, waiting for transfers between devices, local(): value_piece = lax.all_gather(own_values, 'ctx', axis=0, tiled=True)  61.4 us
    unnamed x1, blocking collectives  28.6 us
    dot_general x16, matrix products, attend(): jnp.einsum('hij,jd->hid', exp_terms.astype(jnp.bfloat16), value_piece, pr...  27.7 us
    dot_general x16, matrix products, attend(): jnp.einsum('ihd,jd->hij', soft_rows, key_piece, preferred_element_type=jn...  23.3 us
    ppermute x4, starting transfers between devices, swapped(): lax.ppermute(value, axis, [(i, i ^ 1 << stride) for i in range(lax.axis_s...  16 us
    select_n x17, other arithmetic, doc_index(): return jnp.where(positions < 0, -1, counted)  10.4 us
    add x17, other arithmetic, local(): positions = ctx_place * tok_count + jnp.arange(tok_count, dtype=jnp.int32)  10.4 us
  transfers between devices with their start and end apart: 7, of which 7 were waited for; matrix products, arithmetic and copies ran while one was open for 3% of the time, Pallas kernels for 0%

commit v1 on v0

--- a/solution.py
+++ b/solution.py
@@ -169,7 +169,8 @@
         jnp.zeros((heads_here, tok_count, DH), jnp.float32),
     )
     key_piece = lax.all_gather(own_keys, "ctx", axis=0, tiled=True)
-    value_piece = lax.all_gather(own_values, "ctx", axis=0, tiled=True)
+    copies = jnp.concatenate([own_values] * lax.axis_size("ctx"), axis=0)
+    value_piece = lax.all_to_all(copies, "ctx", 0, 0, tiled=True)
     row_count = key_piece.shape[0]
 
     def inner_visit(state_in, scan_items):

time: 326 us -> 264 us (0.81)
  waiting for transfers between devices: 137 us -> 69.6 us
  starting transfers between devices: 16.2 us -> 20.6 us
    all_gather x1 -> x0, waiting for transfers between devices: 61.4 us -> none  [local(): value_piece = lax.all_gather(own_values, 'ctx', axis=0, tiled=True)]
    ppermute x4, waiting for transfers between devices: 7.79 us -> 1.84 us  [swapped(): lax.ppermute(value, axis, [(i, i ^ 1 << stride) for i in range(lax.axis_s...]
    all_to_all x0 -> x1, starting transfers between devices: none -> 4.56 us  [local(): value_piece = lax.all_to_all(copies, 'ctx', 0, 0, tiled=True)]
    all_gather x1 -> x0, local copies, waits for them, and re-layouts: 4.08 us -> none  [local(): value_piece = lax.all_gather(own_values, 'ctx', axis=0, tiled=True)]
  transfers between devices with their start and end apart: 7 -> 7, of which waited for: 7 -> 3; matrix products, arithmetic and copies ran while one was open for 3% -> 6% of each run, Pallas kernels for 0% -> 0%
where the time goes in v1:
time: 264 us; the launch traced here: 262 us
  waiting for transfers between devices  69.6 us (26%)
  matrix products  53.5 us (20%)
  other arithmetic  44.3 us (17%)
  blocking collectives  28.8 us (11%)
  local copies, waits for them, and re-layouts  25.1 us (10%)
  starting transfers between devices  20.6 us (8%)
  between operations  18.5 us (7%)
    all_gather x1, waiting for transfers between devices, local(): key_piece = lax.all_gather(own_keys, 'ctx', axis=0, tiled=True)  65.2 us
    unnamed x1, blocking collectives  28.8 us
    dot_general x16, matrix products, attend(): jnp.einsum('hij,jd->hid', exp_terms.astype(jnp.bfloat16), value_piece, pr...  27.7 us
    dot_general x16, matrix products, attend(): jnp.einsum('ihd,jd->hij', soft_rows, key_piece, preferred_element_type=jn...  23.3 us
    ppermute x4, starting transfers between devices, swapped(): lax.ppermute(value, axis, [(i, i ^ 1 << stride) for i in range(lax.axis_s...  16 us
    select_n x17, other arithmetic, doc_index(): return jnp.where(positions < 0, -1, counted)  10.4 us
    add x17, other arithmetic, local(): positions = ctx_place * tok_count + jnp.arange(tok_count, dtype=jnp.int32)  10.4 us
    dynamic_slice x16, local copies, waits for them, and re-layouts, local(): lax.scan(inner_visit, start_state, (offsets, key_piece.reshape(row_count...  9.38 us
  transfers between devices with their start and end apart: 7, of which 3 were waited for; matrix products, arithmetic and copies ran while one was open for 6% of the time, Pallas kernels for 0%

profile of v1, /device:TPU:1, one launch (start us, length us, event | category | flops | bytes accessed | tf_op | source)
XLA Modules:
  0.0 261.6 jit_solution(8384571826092822789)
XLA Ops:
  22.6 8.8 %collective-permute-start.2 = (bf16[512,32]{0,1:T(8,128)(2,1)S(1)}, bf16[512,32]{0,1:T(8,128)(2,1)S(1)}, u32[]{:S(2)}, u32[]{:S(2)}) collective-permute-start(bf16[512,32]{0,1:T(8,128)(2,1)S(1)} %copy-done.4), channel_id=1, source_target_pairs={{0,1},{1,0},{2,3},{3,2},{4,5},{5,4},{6,7},{7,6},{8,9},{9,8},{10,11... | collective-permute-start | bytes 98312 | tf_op jit(solution)/shard_map/ppermute | solution.py:32
  31.4 1.9 collective-permute-start
  36.3 28.8 %all-reduce = bf16[32]{0:T(256)(128)(2,1)S(1)} all-reduce(bf16[32]{0:T(256)(128)(2,1)S(1)} %dynamic-update-slice), channel_id=2, replica_groups=mesh['ctx'=16,'head'=32] {'ctx'}, use_global_device_ids=true, to_apply=%add | all-reduce | flops 32 | bytes 128
  66.5 2.8 %collective-permute-start.1 = (bf16[512,64]{0,1:T(8,128)(2,1)S(1)}, bf16[512,64]{0,1:T(8,128)(2,1)S(1)}, u32[]{:S(2)}, u32[]{:S(2)}) collective-permute-start(bf16[512,64]{0,1:T(8,128)(2,1)S(1)} %maximum_select_fusion.2), channel_id=1, source_target_pairs={{0,2},{1,3},{2,0},{3,1},{4,6},{5,7},{6,4},{7,5},{8,10},{9,11},{10,... | collective-permute-start | bytes 196616 | tf_op jit(solution)/shard_map/ppermute | solution.py:32
  69.4 2.5 collective-permute-start.3
  72.6 1.8 collective-permute-done.3
  75.0 2.5 copy.124
  77.4 4.6 %all-to-all-start = ((bf16[16,512,128]{2,1,0:T(8,128)(2,1)}), bf16[16,512,128]{2,1,0:T(8,128)(2,1)}, u32[]{:S(2)}, u32[]{:S(2)}) async-start(bf16[16,512,128]{2,1,0:T(8,128)(2,1)} %bitcast.33), calls=%async_computation | async-start | bytes 4194304 | tf_op jit(solution)/shard_map/all_to_all | solution.py:173
  82.0 2.6 all-gather.7.cloned.1.call-done
  88.1 65.2 %all-gather.5.cloned.1.call-done = bf16[8192,128]{0,1:T(8,128)(2,1)} async-done(((bf16[512,128]{0,1:T(8,128)(2,1)}), bf16[8192,128]{0,1:T(8,128)(2,1)}) %all-gather.5.cloned.1.call-update) | async-done | bytes 2097168 | tf_op jit(solution)/shard_map/all_gather | solution.py:171
  153.3 4.1 %copy.122 = bf16[8192,128]{1,0:T(8,128)(2,1)} copy(bf16[8192,128]{0,1:T(8,128)(2,1)} %all-gather.5.cloned.1.call-done) | data formatting | bytes 4194304 | tf_op jit(solution)/shard_map/all_gather | solution.py:171
  157.4 96.5 %while.30 = (s32[]{:T(128)}, f32[2,512]{1,0:T(2,128)S(1)}, f32[2,512]{1,0:T(2,128)S(1)}, f32[2,512,128]{2,1,0:T(8,128)S(1)}, s32[16]{0:T(128)S(1)}, /*index=5*/s...) while((s32[]{:T(128)}, f32[2,512]{1,0:T(2,128)S(1)}, ...), condition=%wide.region_15.16_spmd.clone, body=%wide.region_11.15_spmd.clone.sunk | while | flops 275395584 | bytes 9000113 | solution.py:181
  161.6 1.7 convolution_add_fusion.3
  165.7 1.5 fusion.92
  167.7 1.7 convolution_add_fusion.3
  173.7 1.7 convolution_add_fusion.3
  179.7 1.7 convolution_add_fusion.3
  183.8 1.5 fusion.92
  185.8 1.7 convolution_add_fusion.3
  191.8 1.7 convolution_add_fusion.3
  197.8 1.7 convolution_add_fusion.3
  201.8 1.5 fusion.92
  203.8 1.7 convolution_add_fusion.3
  209.9 1.7 convolution_add_fusion.3
  215.9 1.7 convolution_add_fusion.3
  219.9 1.5 fusion.92
  221.9 1.7 convolution_add_fusion.3
  228.0 1.7 convolution_add_fusion.3
  234.0 1.7 convolution_add_fusion.3
  240.0 1.7 convolution_add_fusion.3
  246.1 1.7 convolution_add_fusion.3
  252.1 1.7 convolution_add_fusion.3
  (279 shorter events, 82.9 us)
Async XLA Ops:
  7.2 15.4 %copy-start.4 = (bf16[512,32]{0,1:T(8,128)(2,1)S(1)}, bf16[512,32]{0,1:T(8,128)(2,1)}, u32[]{:S(2)}) copy-start(bf16[512,32]{0,1:T(8,128)(2,1)} %param.21) | copy-start | bytes 98308
  7.2 24.2 %copy-start.3 = (bf16[512,32]{0,1:T(8,128)(2,1)S(1)}, bf16[512,32]{0,1:T(8,128)(2,1)}, u32[]{:S(2)}) copy-start(bf16[512,32]{0,1:T(8,128)(2,1)} %param.20) | copy-start | bytes 98308
  7.2 28.5 %copy-start.1 = (bf16[512,256]{1,0:T(8,128)(2,1)S(1)}, bf16[512,256]{1,0:T(8,128)(2,1)}, u32[]{:S(2)}) copy-start(bf16[512,256]{1,0:T(8,128)(2,1)} %param.14) | copy-start | bytes 786436
  7.2 57.9 %copy-start.2 = (bf16[512,256]{1,0:T(8,128)(2,1)S(1)}, bf16[512,256]{1,0:T(8,128)(2,1)}, u32[]{:S(2)}) copy-start(bf16[512,256]{1,0:T(8,128)(2,1)} %param.19) | copy-start | bytes 786436
  7.2 77.4 %all-gather.7.cloned.1.call-start = ((), (), s32[]{:S(2)}) async-start(), calls=%async_computation.2 | async-start | bytes 1114112 | tf_op jit(solution)/shard_map/all_gather | solution.py:14
  16.1 0.6 copy-start.7
  17.8 3.1 %copy-start.9 = (f32[1,2,2,128]{3,1,2,0:T(2,128)}, f32[1,2,2,128]{3,1,2,0:T(2,128)S(1)}, u32[]{:S(2)}) copy-start(f32[1,2,2,128]{3,1,2,0:T(2,128)S(1)} %copy.162) | copy-start | bytes 6148
  19.0 46.4 %copy-start.13 = (s32[4]{0:T(128)S(1)}, s32[4]{0:T(128)}, u32[]{:S(2)}) copy-start(s32[4]{0:T(128)} %param.13) | copy-start | bytes 52
  22.5 130.7 %all-gather.5.cloned.1.call-start = ((), (), s32[]{:S(2)}) async-start(), calls=%async_computation.1 | async-start | bytes 2228224 | tf_op jit(solution)/shard_map/all_gather | solution.py:171
  22.6 46.8 %collective-permute-start.2 = (bf16[512,32]{0,1:T(8,128)(2,1)S(1)}, bf16[512,32]{0,1:T(8,128)(2,1)S(1)}, u32[]{:S(2)}, u32[]{:S(2)}) collective-permute-start(bf16[512,32]{0,1:T(8,128)(2,1)S(1)} %copy-done.4), channel_id=1, source_target_pairs={{0,1},{1,0},{2,3},{3,2},{4,5},{5,4},{6,7},{7,6},{8,9},{9,8},{10,11... | collective-permute-start | bytes 98312 | tf_op jit(solution)/shard_map/ppermute | solution.py:32
  31.4 35.1 %collective-permute-start = (bf16[512,32]{0,1:T(8,128)(2,1)S(1)}, bf16[512,32]{0,1:T(8,128)(2,1)S(1)}, u32[]{:S(2)}, u32[]{:S(2)}) collective-permute-start(bf16[512,32]{0,1:T(8,128)(2,1)S(1)} %copy-done.3), channel_id=1, source_target_pairs={{0,1},{1,0},{2,3},{3,2},{4,5},{5,4},{6,7},{7,6},{8,9},{9,8},{10,11... | collective-permute-start | bytes 98312 | tf_op jit(solution)/shard_map/ppermute | solution.py:32
  66.5 5.3 %collective-permute-start.1 = (bf16[512,64]{0,1:T(8,128)(2,1)S(1)}, bf16[512,64]{0,1:T(8,128)(2,1)S(1)}, u32[]{:S(2)}, u32[]{:S(2)}) collective-permute-start(bf16[512,64]{0,1:T(8,128)(2,1)S(1)} %maximum_select_fusion.2), channel_id=1, source_target_pairs={{0,2},{1,3},{2,0},{3,1},{4,6},{5,7},{6,4},{7,5},{8,10},{9,11},{10,... | collective-permute-start | bytes 196616 | tf_op jit(solution)/shard_map/ppermute | solution.py:32
  69.4 5.0 %collective-permute-start.3 = (bf16[512,64]{0,1:T(8,128)(2,1)S(1)}, bf16[512,64]{0,1:T(8,128)(2,1)S(1)}, u32[]{:S(2)}, u32[]{:S(2)}) collective-permute-start(bf16[512,64]{0,1:T(8,128)(2,1)S(1)} %maximum_select_fusion.3), channel_id=1, source_target_pairs={{0,2},{1,3},{2,0},{3,1},{4,6},{5,7},{6,4},{7,5},{8,10},{9,11},{10,... | collective-permute-start | bytes 196616 | tf_op jit(solution)/shard_map/ppermute | solution.py:32
  77.4 7.2 %copy-start.6 = (f32[256,2]{0,1:T(2,128)S(1)}, f32[256,2]{0,1:T(2,128)}, u32[]{:S(2)}) copy-start(f32[256,2]{0,1:T(2,128)} %get-tuple-element.310) | copy-start | bytes 6148
  77.4 79.9 %all-to-all-start = ((bf16[16,512,128]{2,1,0:T(8,128)(2,1)}), bf16[16,512,128]{2,1,0:T(8,128)(2,1)}, u32[]{:S(2)}, u32[]{:S(2)}) async-start(bf16[16,512,128]{2,1,0:T(8,128)(2,1)} %bitcast.33), calls=%async_computation | async-start | bytes 4194304 | tf_op jit(solution)/shard_map/all_to_all | solution.py:173
  82.0 2.9 %copy-start.5 = (f32[256,2]{0,1:T(2,128)S(1)}, f32[256,2]{0,1:T(2,128)}, u32[]{:S(2)}) copy-start(f32[256,2]{0,1:T(2,128)} %get-tuple-element.320) | copy-start | bytes 6148
  82.0 2.9 %copy-start.11 = (f32[2]{0:T(128)S(1)}, f32[2]{0:T(128)}, u32[]{:S(2)}) copy-start(f32[2]{0:T(128)} %get-tuple-element.295) | copy-start | bytes 28
  82.0 3.2 %copy-start.10 = (f32[1,2,2,128]{3,1,2,0:T(2,128)S(1)}, f32[1,2,2,128]{3,1,2,0:T(2,128)}, u32[]{:S(2)}) copy-start(f32[1,2,2,128]{3,1,2,0:T(2,128)} %copy-done.9) | copy-start | bytes 6148
  84.7 1.1 copy-start.8
  85.7 1.6 copy-start.12
  88.1 69.3 %copy-start = (f32[2,512,128]{2,1,0:T(8,128)S(1)}, f32[2,512,128]{2,1,0:T(8,128)}, u32[]{:S(2)}) copy-start(f32[2,512,128]{2,1,0:T(8,128)} %custom-call.2) | copy-start | bytes 1572868
  88.1 69.3 %copy-start.14 = (s32[16]{0:T(128)S(1)}, s32[16]{0:T(128)}, u32[]{:S(2)}) copy-start(s32[16]{0:T(128)} %iota_multiply_fusion) | copy-start | bytes 196
Sparse Core Ops, SparseCore 0:
  22.7 61.9 all-gather.6
  88.2 65.0 all-gather.4
